TPU v7x, 32 devices: a whole 2x2x4 slice. The times are simulated.
32 devices in a mesh: rows: 4 (over y, x), seq: 8 (over z, core).
Axes of the slice: x: 2, y: 2, z: 4, core: 2. Of those that a mesh axis runs over, the one named last changes fastest.
Arguments:
- residual_in: float32 [32, 1024, 512], P('rows', 'seq'), may hold values from -6 to 6
- cotangent: float32 [32, 1024, 512], P('rows', 'seq'), may hold values from -6 to 6
- segments: int32 [32, 1024], P('rows'), may hold values from 0 to 7, never falling along the last dimension, each value on 1 to 512 neighbouring positions
- owners: int32 [96], replicated, may hold values from 0 to 7, as said below
- master_tiles: float32 [128, 512, 128], P('seq'), may hold values from -0.53033009 to 0.53033009, as said below
- first_tiles: float32 [128, 512, 128], P('seq'), may hold values from -0.0024414062 to 0.0024414062
- second_tiles: float32 [128, 512, 128], P('seq'), may hold values from 1.5873903e-07 to 6.349561e-07
- norm_params: float32 [8, 512], replicated, may hold values from -2 to 2
- norm_first: float32 [8, 512], replicated, may hold values from -0.009765625 to 0.009765625
- norm_second: float32 [8, 512], replicated, may hold values from 2.5398244e-06 to 1.0159298e-05
Outputs:
- residual_out: float32 [32, 1024, 512], P('rows', 'seq')
- input_grad: float32 [32, 1024, 512], P('rows', 'seq')
- tile_grads: float32 [128, 512, 128], P('seq')
- grad_norm: float32 [1], replicated
- new_first: float32 [128, 512, 128], P('seq')
- new_second: float32 [128, 512, 128], P('seq')
- new_master: float32 [128, 512, 128], P('seq')
- new_copies: bfloat16 [128, 512, 128], P('seq')
- norm_grads: float32 [8, 512], replicated
- new_norm_first: float32 [8, 512], replicated
- new_norm_second: float32 [8, 512], replicated
- new_norm_params: float32 [8, 512], replicated
Inputs may be any that keep to these rules, and one draw needn't show every extreme that they name: `owners`: no device owns more than 16 tiles, and one device owns exactly 16. `segments`: along a row the document numbers never fall; a document has 1 to 512 positions and some document exactly 512. `master_tiles`: slot 16 d + n holds the tile with the n-th smallest number among those owned by device d; slots that hold no tile are ignored.
All inputs are finite; a program needn't handle non-finite values.
Results may differ from a plain program's by a relative error of at most 0.013.
Values may be sent and summed in bfloat16 or wider, within the bound.
A program may use at most 256 MiB of HBM per device.

v0:
```python
import jax
import jax.numpy as jnp
from jax import lax
from jax.sharding import PartitionSpec as P

HEADS = 8
LAYERS = 2
STEP = 5


def norm_layer(values, gain, offset):
    center = values - jnp.mean(values, axis=-1, keepdims=True)
    spread = jnp.mean(center * center, axis=-1, keepdims=True)
    return center * lax.rsqrt(spread + 1e-05) * gain + offset


def matmul(left, right):
    return jnp.dot(left, right, preferred_element_type=jnp.float32)


def left_product(left, right):
    return lax.dot_general(
        left, right, (((0,), (0,)), ((), ())), preferred_element_type=jnp.float32
    )


def right_product(left, right):
    return lax.dot_general(
        left, right, (((1,), (1,)), ((), ())), preferred_element_type=jnp.float32
    )


def assemble(weight_tiles, layer_number):
    first_tile = 48 * layer_number
    model_width = weight_tiles.shape[1]
    qkv_weight = (
        weight_tiles[first_tile : first_tile + 12].transpose(1, 0, 2).reshape(model_width, -1)
    )
    out_weight = (
        weight_tiles[first_tile + 12 : first_tile + 16].transpose(1, 0, 2).reshape(model_width, -1)
    )
    up_weight = (
        weight_tiles[first_tile + 16 : first_tile + 32].transpose(1, 0, 2).reshape(model_width, -1)
    )
    down_block = weight_tiles[first_tile + 32 : first_tile + 48].reshape(4, 4, model_width, -1)
    down_weight = down_block.transpose(0, 2, 1, 3).reshape(4 * model_width, model_width)
    return (qkv_weight, out_weight, up_weight, down_weight)


def split_tiles(qkv_grad, out_grad, up_grad, down_grad, tile_width):
    model_width = qkv_grad.shape[0]
    pieces = [
        qkv_grad.reshape(model_width, -1, tile_width).transpose(1, 0, 2),
        out_grad.reshape(model_width, -1, tile_width).transpose(1, 0, 2),
        up_grad.reshape(model_width, -1, tile_width).transpose(1, 0, 2),
        down_grad.reshape(4, model_width, 4, tile_width)
        .transpose(0, 2, 1, 3)
        .reshape(16, model_width, tile_width),
    ]
    return jnp.concatenate(pieces, axis=0)


def attend_forward(queries, key_rows, value_rows, doc_ids, block_rows, scale):
    length = queries.shape[0]

    def one_block(number):
        first_row = number * block_rows
        query_block = lax.dynamic_slice_in_dim(queries, first_row, block_rows, 0)
        doc_block = lax.dynamic_slice_in_dim(doc_ids, first_row, block_rows, 0)
        same_doc = doc_block[:, None] == doc_ids[None, :]
        scores = jnp.where(same_doc, right_product(query_block, key_rows) * scale, -1e30)
        largest = jnp.max(scores, axis=-1, keepdims=True)
        row_total = jnp.sum(jnp.exp(scores - largest), axis=-1, keepdims=True)
        logsum = largest + jnp.log(row_total)
        weights = jnp.where(same_doc, jnp.exp(scores - logsum), 0.0).astype(jnp.bfloat16)
        return (matmul(weights, value_rows).astype(jnp.bfloat16), logsum[:, 0])

    outputs, logsums = lax.map(one_block, jnp.arange(length // block_rows))
    return (outputs.reshape(length, -1), logsums.reshape(length))


def attend_backward(queries, key_rows, value_rows, doc_ids, logsums, out_grads, block_rows, scale):
    length, head_dim = queries.shape

    def one_block(carry, number):
        key_grad, value_grad = carry
        first_row = number * block_rows
        query_block = lax.dynamic_slice_in_dim(queries, first_row, block_rows, 0)
        doc_block = lax.dynamic_slice_in_dim(doc_ids, first_row, block_rows, 0)
        logsum_block = lax.dynamic_slice_in_dim(logsums, first_row, block_rows, 0)
        grad_block = lax.dynamic_slice_in_dim(out_grads, first_row, block_rows, 0)
        same_doc = doc_block[:, None] == doc_ids[None, :]
        scores = jnp.where(same_doc, right_product(query_block, key_rows) * scale, -1e30)
        probs = jnp.where(same_doc, jnp.exp(scores - logsum_block[:, None]), 0.0)
        prob_grad = right_product(grad_block, value_rows)
        inner_sum = jnp.sum(probs * prob_grad, axis=-1, keepdims=True)
        score_grad = (probs * (prob_grad - inner_sum)).astype(jnp.bfloat16)
        query_grad = matmul(score_grad, key_rows) * scale
        key_grad = key_grad + left_product(score_grad, query_block) * scale
        value_grad = value_grad + left_product(probs.astype(jnp.bfloat16), grad_block)
        return ((key_grad, value_grad), query_grad)

    zeros_block = jnp.zeros((length, head_dim), jnp.float32)
    (key_grad, value_grad), query_grads = lax.scan(
        one_block, (zeros_block, zeros_block), jnp.arange(length // block_rows)
    )
    stacked = jnp.stack([query_grads.reshape(length, head_dim), key_grad, value_grad], axis=1)
    return stacked.astype(jnp.bfloat16)


def adamw(weight, grad, first, second, learn_rate, correction):
    first = 0.5 * first + 0.5 * grad
    second = 0.5 * second + 0.5 * grad * grad
    update = first / correction / (jnp.sqrt(second / correction) + 1e-08)
    return (weight - learn_rate * (update + 0.01 * weight), first, second)


def local(
    residual_in,
    cotangent,
    segments,
    owners,
    master_tiles,
    first_tiles,
    second_tiles,
    norm_params,
    norm_first,
    norm_second,
):
    local_rows, positions, model_width = residual_in.shape
    seq_devices = lax.axis_size("seq")
    seq_index = lax.axis_index("seq")
    head_dim = model_width // HEADS
    group_count = seq_devices // HEADS
    group_rows = local_rows // group_count
    length = positions * seq_devices
    block_rows = min(512, length)
    scale = head_dim ** (-0.5)
    tile_total = owners.shape[0]
    capacity = master_tiles.shape[0]
    tile_width = master_tiles.shape[2]
    places = jnp.arange(tile_total, dtype=jnp.int32)
    before = (owners[None, :] == owners[:, None]) & (places[None, :] < places[:, None])
    ranks = jnp.sum(before.astype(jnp.int32), axis=1)
    slot_ids = owners * capacity + ranks
    local_slots = jnp.arange(capacity, dtype=jnp.int32)
    matches = (owners[:, None] == seq_index) & (ranks[:, None] == local_slots[None, :])
    chosen = jnp.sum(jnp.where(matches, places[:, None], 0), axis=0)
    present = jnp.any(matches, axis=0)
    copies = lax.all_gather(master_tiles.astype(jnp.bfloat16), "seq", axis=0, tiled=True)
    weight_tiles = jnp.take(copies, slot_ids, axis=0)
    my_group = seq_index // HEADS
    doc_rows = lax.dynamic_slice_in_dim(segments, my_group * group_rows, group_rows, 0)
    hidden = residual_in.reshape(-1, model_width)
    saved = []
    for layer_number in range(LAYERS):
        qkv_weight, out_weight, up_weight, down_weight = assemble(weight_tiles, layer_number)
        params = norm_params[4 * layer_number : 4 * layer_number + 4]
        normed, first_pull = jax.vjp(norm_layer, hidden, params[0], params[1])
        normed_low = normed.astype(jnp.bfloat16)
        packed = matmul(normed_low, qkv_weight).astype(jnp.bfloat16)
        outgoing = packed.reshape(group_count, group_rows, positions, 3, HEADS, head_dim)
        outgoing = outgoing.transpose(0, 4, 1, 2, 3, 5).reshape(
            seq_devices, group_rows, positions * 3 * head_dim
        )
        arrived = lax.all_to_all(outgoing, "seq", split_axis=0, concat_axis=2, tiled=True).reshape(
            group_rows, length, 3, head_dim
        )

        def forward_item(items):
            return attend_forward(
                items[0][:, 0], items[0][:, 1], items[0][:, 2], items[1], block_rows, scale
            )

        attended, logsums = lax.map(forward_item, (arrived, doc_rows))
        returning = attended.reshape(1, group_rows, seq_devices, positions * head_dim)
        mixed = lax.all_to_all(returning, "seq", split_axis=2, concat_axis=0, tiled=True)
        mixed = (
            mixed.reshape(group_count, HEADS, group_rows, positions, head_dim)
            .transpose(0, 2, 3, 1, 4)
            .reshape(-1, model_width)
        )
        middle = hidden + matmul(mixed, out_weight)
        normed_two, second_pull = jax.vjp(norm_layer, middle, params[2], params[3])
        normed_two_low = normed_two.astype(jnp.bfloat16)
        inner = matmul(normed_two_low, up_weight)
        active = jax.nn.gelu(inner).astype(jnp.bfloat16)
        hidden = middle + matmul(active, down_weight)
        saved.append(
            (
                first_pull,
                normed_low,
                arrived,
                logsums,
                mixed,
                second_pull,
                normed_two_low,
                inner,
                active,
            )
        )
    grad = cotangent.reshape(-1, model_width)
    tile_parts = [None] * LAYERS
    norm_parts = [None] * LAYERS
    for layer_number in reversed(range(LAYERS)):
        (
            first_pull,
            normed_low,
            arrived,
            logsums,
            mixed,
            second_pull,
            normed_two_low,
            inner,
            active,
        ) = saved[layer_number]
        qkv_weight, out_weight, up_weight, down_weight = assemble(weight_tiles, layer_number)
        grad_low = grad.astype(jnp.bfloat16)
        down_grad = left_product(active, grad_low)
        active_grad = right_product(grad_low, down_weight)
        inner_grad = jax.vjp(jax.nn.gelu, inner)[1](active_grad)[0].astype(jnp.bfloat16)
        up_grad = left_product(normed_two_low, inner_grad)
        middle_part, gain_two, offset_two = second_pull(right_product(inner_grad, up_weight))
        middle_grad = grad + middle_part
        middle_low = middle_grad.astype(jnp.bfloat16)
        out_grad = left_product(mixed, middle_low)
        mixed_grad = right_product(middle_low, out_weight).astype(jnp.bfloat16)
        sending = mixed_grad.reshape(group_count, group_rows, positions, HEADS, head_dim)
        sending = sending.transpose(0, 3, 1, 2, 4).reshape(
            seq_devices, group_rows, positions * head_dim
        )
        head_grads = lax.all_to_all(
            sending, "seq", split_axis=0, concat_axis=2, tiled=True
        ).reshape(group_rows, length, head_dim)

        def backward_item(items):
            arrived_row, doc_row, logsum_row, grad_row = items
            return attend_backward(
                arrived_row[:, 0],
                arrived_row[:, 1],
                arrived_row[:, 2],
                doc_row,
                logsum_row,
                grad_row,
                block_rows,
                scale,
            )

        packed_grads = lax.map(backward_item, (arrived, doc_rows, logsums, head_grads))
        coming = lax.all_to_all(
            packed_grads.reshape(1, group_rows, seq_devices, positions * 3 * head_dim),
            "seq",
            split_axis=2,
            concat_axis=0,
            tiled=True,
        )
        qkv_grad = coming.reshape(group_count, HEADS, group_rows, positions, 3, head_dim)
        qkv_grad = qkv_grad.transpose(0, 2, 3, 4, 1, 5).reshape(-1, 3 * model_width)
        qkv_weight_grad = left_product(normed_low, qkv_grad)
        input_part, gain_one, offset_one = first_pull(right_product(qkv_grad, qkv_weight))
        grad = middle_grad + input_part
        tile_parts[layer_number] = split_tiles(
            qkv_weight_grad, out_grad, up_grad, down_grad, tile_width
        )
        norm_parts[layer_number] = jnp.stack([gain_one, offset_one, gain_two, offset_two])
    dense = jnp.concatenate(tile_parts, axis=0)
    norm_part = jnp.concatenate(norm_parts, axis=0)
    piece = lax.psum_scatter(
        dense.reshape(-1, tile_width), ("rows", "seq"), scatter_dimension=0, tiled=True
    )
    squares, norm_sum = lax.psum((jnp.sum(piece * piece), norm_part), ("rows", "seq"))
    summed = (
        lax.all_gather(piece.astype(jnp.bfloat16), ("rows", "seq"), axis=0, tiled=True)
        .astype(piece.dtype)
        .reshape(dense.shape)
    )
    owned = jnp.take(summed, chosen, axis=0)
    keep = present[:, None, None]
    owned = jnp.where(keep, owned, 0.0)
    total = jnp.sqrt(squares + jnp.sum(norm_sum * norm_sum))
    factor = 1.0 / jnp.maximum(total, 1.0)
    clipped = owned * factor
    norm_clip = norm_sum * factor
    correction = 1.0 - 0.5**STEP
    new_weight, new_first_rows, new_second_rows = adamw(
        master_tiles, clipped, first_tiles, second_tiles, 0.05, correction
    )
    new_weight = jnp.where(keep, new_weight, 0.0)
    new_first_rows = jnp.where(keep, new_first_rows, 0.0)
    new_second_rows = jnp.where(keep, new_second_rows, 0.0)
    new_norm, new_norm_f, new_norm_s = adamw(
        norm_params, norm_clip, norm_first, norm_second, 0.25, correction
    )
    return (
        hidden.reshape(local_rows, positions, model_width),
        grad.reshape(local_rows, positions, model_width),
        clipped,
        total[None],
        new_first_rows,
        new_second_rows,
        new_weight,
        new_weight.astype(jnp.bfloat16),
        norm_clip,
        new_norm_f,
        new_norm_s,
        new_norm,
    )


def solution(mesh):
    placed = (
        P("rows", "seq", None),
        P("rows", "seq", None),
        P("rows", None),
        P(),
        P("seq", None, None),
        P("seq", None, None),
        P("seq", None, None),
        P(),
        P(),
        P(),
    )
    return jax.shard_map(
        local,
        mesh=mesh,
        in_specs=placed,
        out_specs=(
            P("rows", "seq", None),
            P("rows", "seq", None),
            P("seq", None, None),
            P(),
            P("seq", None, None),
            P("seq", None, None),
            P("seq", None, None),
            P("seq", None, None),
            P(),
            P(),
            P(),
            P(),
        ),
        check_vma=False,
    )
```

profile of v0, /device:TPU:0, one launch (start us, length us, event | category | flops | bytes accessed | tf_op | source)
XLA Modules:
  0.0 1696.8 jit_solution(15735014790983426228)
XLA Ops:
  17.2 147.9 %all-gather.3.cloned.1.call-done = bf16[128,512,128]{2,1,0:T(8,128)(2,1)} async-done(((bf16[16,512,128]{2,1,0:T(8,128)(2,1)}), bf16[128,512,128]{2,1,0:T(8,128)(2,1)}) %all-gather.3.cloned.1.call-update) | async-done | bytes 16777232 | tf_op jit(solution)/shard_map/all_gather | solution.py:150
  165.1 12.7 gather_fusion
  177.8 6.5 broadcast_select_fusion
  202.6 9.9 copy.210
  212.6 10.4 reshape.599
  226.8 71.4 %all-to-all-done = bf16[8,8,24576]{2,1,0:T(8,128)(2,1)S(1)} async-done(((bf16[8,8,24576]{2,1,0:T(8,128)(2,1)}), bf16[8,8,24576]{2,1,0:T(8,128)(2,1)S(1)}, u32[]{:S(2)}, u32[]{:S(2)}) %all-to-all-start) | async-done | bytes 3145760 | tf_op jit(solution)/shard_map/all_to_all | solution.py:166
  301.6 10.4 reshape.600
  312.1 7.7 copy.212
  320.5 63.0 %while.99 = (s32[]{:T(128)}, bf16[8,1024,64]{2,1,0:T(8,128)(2,1)S(1)}, f32[8,1024]{1,0:T(8,128)S(1)}, bf16[8,1024,3,64]{3,1,2,0:T(8,128)(2,1)}, s32[8,1024]{1,0:...) while((s32[]{:T(128)}, ...), condition=%wide.region_8.9_spmd, body=%wide.region_3.8_spmd.sunk | while | flops 139492864 | bytes 9431484 | solution.py:175
  448.7 10.0 copy.220
  458.7 10.4 reshape.610
  473.9 71.5 %all-to-all-done.2 = bf16[8,8,24576]{2,1,0:T(8,128)(2,1)} async-done(((bf16[8,8,24576]{2,1,0:T(8,128)(2,1)}), bf16[8,8,24576]{2,1,0:T(8,128)(2,1)}, u32[]{:S(2)}, u32[]{:S(2)}) %all-to-all-start.2) | async-done | bytes 3145760 | tf_op jit(solution)/shard_map/all_to_all | solution.py:166
  550.8 10.5 reshape.611
  561.2 7.7 copy.222
  570.5 69.8 %while.101 = (s32[]{:T(128)}, bf16[8,1024,64]{2,1,0:T(8,128)(2,1)}, f32[8,1024]{1,0:T(8,128)S(1)}, bf16[8,1024,3,64]{3,1,2,0:T(8,128)(2,1)}, s32[8,1024]{1,0:T(8...) while((s32[]{:T(128)}, bf16[8,1024,64]{2,1,0:T(8,128)(2,1)}, ...), condition=%wide.region_18.19_spmd, body=%wide.region_13.18_spmd.sunk | while | flops 139492864 | bytes 9300412 | solution.py:175
  571.8 6.4 while.107
  580.5 6.4 while.107
  589.2 6.4 while.107
  606.7 6.4 while.107
  615.4 6.4 while.107
  665.0 10.4 all-to-all-done.3
  685.3 6.5 fusion.71
  691.8 7.9 fusion.63
  715.4 26.5 %all-to-all-done.4 = bf16[8,8,8192]{2,1,0:T(8,128)(2,1)S(1)} async-done(((bf16[8,8,8192]{2,1,0:T(8,128)(2,1)}), bf16[8,8,8192]{2,1,0:T(8,128)(2,1)S(1)}, u32[]{:S(2)}, u32[]{:S(2)}) %all-to-all-start.4) | async-done | bytes 1048608 | tf_op jit(solution)/shard_map/all_to_all | solution.py:232
  748.7 104.2 %while.103 = (s32[]{:T(128)}, bf16[8,1024,3,64]{1,3,2,0:T(8,128)(2,1)}, bf16[8,1024,3,64]{3,1,2,0:T(8,128)(2,1)}, s32[8,1024]{1,0:T(8,128)S(1)}, f32[8,1024]{1,0...) while((s32[]{:T(128)}, ...), condition=%wide.region_27.28_spmd, body=%wide.region_23.27_spmd.sunk | while | flops 342982144 | bytes 30577220 | solution.py:249
  751.3 8.7 while.108
  764.3 8.7 while.108
  777.3 8.7 while.108
  790.4 8.7 while.108
  803.4 8.7 while.108
  816.4 8.7 while.108
  829.4 8.7 while.108
  842.4 8.7 while.108
  852.9 12.5 copy.235
  865.4 9.2 reshape.624
  876.4 74.5 %all_to_all.120 = bf16[1,8,8,24576]{3,1,0,2:T(8,128)(2,1)S(1)} all-to-all(bf16[1,8,8,24576]{3,1,0,2:T(8,128)(2,1)S(1)} %copy.236), channel_id=1, replica_groups=mesh['rows'=4,'seq'=8] {'seq'}, dimensions={2} | all-to-all | bytes 6291456 | tf_op jit(solution)/shard_map/all_to_all | solution.py:250
  950.8 8.7 reshape.625
  959.5 8.0 copy.237
  983.5 10.4 fusion.56
  1016.3 26.5 %all-to-all-done.6 = bf16[8,8,8192]{2,1,0:T(8,128)(2,1)S(1)} async-done(((bf16[8,8,8192]{2,1,0:T(8,128)(2,1)}), bf16[8,8,8192]{2,1,0:T(8,128)(2,1)S(1)}, u32[]{:S(2)}, u32[]{:S(2)}) %all-to-all-start.6) | async-done | bytes 1048608 | tf_op jit(solution)/shard_map/all_to_all | solution.py:232
  1049.6 102.7 %while.105 = (s32[]{:T(128)}, bf16[8,1024,3,64]{1,3,2,0:T(8,128)(2,1)}, bf16[8,1024,3,64]{3,1,2,0:T(8,128)(2,1)}, s32[8,1024]{1,0:T(8,128)S(1)}, f32[8,1024]{1,0...) while((s32[]{:T(128)}, ...), condition=%wide.region_36.37_spmd, body=%wide.region_32.36_spmd.sunk | while | flops 342982144 | bytes 30577220 | solution.py:249
  1052.2 8.5 while.109
  1065.1 8.5 while.109
  1077.9 8.5 while.109
  1090.7 8.5 while.109
  1103.6 8.5 while.109
  1116.4 8.5 while.109
  1129.3 8.5 while.109
  1142.1 8.5 while.109
  1152.4 12.5 copy.244
  1164.9 9.2 reshape.630
  1184.2 6.5 copy.267
  1190.8 6.9 convolution_bitcast_fusion
  1200.3 9.2 fusion.106
  1228.1 25.8 %all-to-all-done.7 = bf16[1,8,8,24576]{3,1,0,2:T(8,128)(2,1)} async-done(((bf16[1,8,8,24576]{3,1,0,2:T(8,128)(2,1)}), bf16[1,8,8,24576]{3,1,0,2:T(8,128)(2,1)}, u32[]{:S(2)}, u32[]{:S(2)}) %all-to-all-start.7) | async-done | bytes 3145760 | tf_op jit(solution)/shard_map/all_to_all | solution.py:250
  1253.9 10.6 reshape.631
  1264.4 9.5 copy.246
  1302.8 244.3 %reduce-scatter.2.cloned.1.call-done = f32[1536,128]{1,0:T(8,128)} async-done(((f32[49152,128]{1,0:T(8,128)}), f32[1536,128]{1,0:T(8,128)}) %reduce-scatter.2.cloned.1.call-update) | async-done | bytes 786448 | tf_op jit(solution)/shard_map/reduce_scatter | solution.py:268
  1550.3 8.7 fusion.91
  1579.6 42.8 %all-reduce = (f32[]{:T(128)}, f32[8,512]{1,0:T(8,128)S(1)}) all-reduce(f32[]{:T(128)} %get-tuple-element.743, f32[8,512]{1,0:T(8,128)S(1)} %concatenate.23), channel_id=1, replica_groups=mesh['rows'=4,'seq'=8] {'rows','seq'}, use_global_device_ids=true, to_apply=%region_43.44 | all-reduce | flops 4097 | bytes 32776 | tf_op jit(solution)/shard_map/psum | solution.py:271
  1625.1 23.5 %all-gather.5.cloned.1.call-done = bf16[49152,128]{1,0:T(8,128)(2,1)} async-done(((bf16[1536,128]{1,0:T(8,128)(2,1)}), bf16[49152,128]{1,0:T(8,128)(2,1)}) %all-gather.5.cloned.1.call-update) | async-done | bytes 12582928 | tf_op jit(solution)/shard_map/all_gather | solution.py:273
  1648.5 14.2 convert.25
  1662.7 11.0 gather_fusion.1
  1673.7 9.6 fusion.133
  (1344 shorter events, 667.7 us)
Async XLA Ops:
  7.2 157.9 %all-gather.3.cloned.1.call-start = ((), (), s32[]{:S(2)}) async-start(), calls=%async_computation.9 | async-start | bytes 18874368 | tf_op jit(solution)/shard_map/all_gather | solution.py:150
  15.3 410.2 %copy-start.97 = (f32[1,512]{1,0:T(1,128)}, f32[1,512]{1,0:T(1,128)S(1)}, u32[]{:S(2)}) copy-start(f32[1,512]{1,0:T(1,128)S(1)} %get-tuple-element.748) | copy-start | bytes 6148
  15.3 410.2 %copy-start.110 = (f32[1,512]{1,0:T(1,128)}, f32[1,512]{1,0:T(1,128)S(1)}, u32[]{:S(2)}) copy-start(f32[1,512]{1,0:T(1,128)S(1)} %get-tuple-element.747) | copy-start | bytes 6148
  15.3 418.9 %copy-start.94 = (f32[1,512]{1,0:T(1,128)}, f32[1,512]{1,0:T(1,128)S(1)}, u32[]{:S(2)}) copy-start(f32[1,512]{1,0:T(1,128)S(1)} %get-tuple-element.746) | copy-start | bytes 6148
  15.3 418.9 %copy-start.108 = (f32[1,512]{1,0:T(1,128)}, f32[1,512]{1,0:T(1,128)S(1)}, u32[]{:S(2)}) copy-start(f32[1,512]{1,0:T(1,128)S(1)} %get-tuple-element.745) | copy-start | bytes 6148
  184.3 4.6 copy-start.5
  222.9 75.3 %all-to-all-start = ((bf16[8,8,24576]{2,1,0:T(8,128)(2,1)}), bf16[8,8,24576]{2,1,0:T(8,128)(2,1)S(1)}, u32[]{:S(2)}, u32[]{:S(2)}) async-start(bf16[8,8,24576]{2,1,0:T(8,128)(2,1)} %reshape.599), calls=%async_computation | async-start | bytes 6291456 | tf_op jit(solution)/shard_map/all_to_all | solution.py:166
  387.4 30.1 %all-to-all-start.1 = ((bf16[1,8,8,8192]{3,1,0,2:T(8,128)(2,1)}), bf16[1,8,8,8192]{3,1,0,2:T(8,128)(2,1)S(1)}, u32[]{:S(2)}, u32[]{:S(2)}) async-start(bf16[1,8,8,8192]{3,1,0,2:T(8,128)(2,1)} %copy.213), calls=%async_computation.1 | async-start | bytes 2097152 | tf_op jit(solution)/shard_map/all_to_all | solution.py:177
  392.9 30.1 %copy-start = (f32[1024,512]{0,1:T(8,128)}, f32[1024,512]{0,1:T(8,128)S(1)}, u32[]{:S(2)}) copy-start(f32[1024,512]{0,1:T(8,128)S(1)} %copy.262) | copy-start | bytes 6291460
  425.1 5.1 copy-start.7
  425.1 5.0 copy-start.71
  425.5 4.7 copy-start.79
  425.5 4.7 copy-start.91
  433.8 247.0 %copy-start.2 = (f32[1024,512]{0,1:T(8,128)}, f32[1024,512]{0,1:T(8,128)S(1)}, u32[]{:S(2)}) copy-start(f32[1024,512]{0,1:T(8,128)S(1)} %get-tuple-element.760) | copy-start | bytes 6291460
  433.8 5.9 copy-start.64
  434.1 5.6 copy-start.81
  434.1 5.6 copy-start.76
  469.1 76.4 %all-to-all-start.2 = ((bf16[8,8,24576]{2,1,0:T(8,128)(2,1)}), bf16[8,8,24576]{2,1,0:T(8,128)(2,1)}, u32[]{:S(2)}, u32[]{:S(2)}) async-start(bf16[8,8,24576]{2,1,0:T(8,128)(2,1)} %reshape.610), calls=%async_computation.2 | async-start | bytes 6291456 | tf_op jit(solution)/shard_map/all_to_all | solution.py:166
  645.2 30.2 %all-to-all-start.3 = ((bf16[1,8,8,8192]{3,1,0,2:T(8,128)(2,1)}), bf16[1,8,8,8192]{3,1,0,2:T(8,128)(2,1)S(1)}, u32[]{:S(2)}, u32[]{:S(2)}) async-start(bf16[1,8,8,8192]{3,1,0,2:T(8,128)(2,1)} %copy.223), calls=%async_computation.3 | async-start | bytes 2097152 | tf_op jit(solution)/shard_map/all_to_all | solution.py:177
  682.9 20.3 %copy-start.12 = (f32[1024,512]{0,1:T(8,128)}, f32[1024,512]{0,1:T(8,128)S(1)}, u32[]{:S(2)}) copy-start(f32[1024,512]{0,1:T(8,128)S(1)} %get-tuple-element.762) | copy-start | bytes 6291460
  682.9 20.2 %copy-start.85 = (f32[1024]{0:T(1024)}, f32[1024]{0:T(1024)S(1)}, u32[]{:S(2)}) copy-start(f32[1024]{0:T(1024)S(1)} %broadcast_multiply_fusion.1) | copy-start | bytes 12292
  683.3 19.9 %copy-start.102 = (f32[1024]{0:T(1024)}, f32[1024]{0:T(1024)S(1)}, u32[]{:S(2)}) copy-start(f32[1024]{0:T(1024)S(1)} %fusion.118) | copy-start | bytes 12292
  685.3 6.5 copy-start.47
  685.3 6.5 copy-start.56
  691.8 7.9 copy-start.126
  711.5 30.3 %all-to-all-start.4 = ((bf16[8,8,8192]{2,1,0:T(8,128)(2,1)}), bf16[8,8,8192]{2,1,0:T(8,128)(2,1)S(1)}, u32[]{:S(2)}, u32[]{:S(2)}) async-start(bf16[8,8,8192]{2,1,0:T(8,128)(2,1)} %reshape.622), calls=%async_computation.4 | async-start | bytes 2097152 | tf_op jit(solution)/shard_map/all_to_all | solution.py:232
  967.5 6.3 copy-start.29
  983.5 10.4 copy-start.21
  983.5 10.4 copy-start.49
  993.9 4.2 copy-start.124
  1012.7 30.1 %all-to-all-start.6 = ((bf16[8,8,8192]{2,1,0:T(8,128)(2,1)}), bf16[8,8,8192]{2,1,0:T(8,128)(2,1)S(1)}, u32[]{:S(2)}, u32[]{:S(2)}) async-start(bf16[8,8,8192]{2,1,0:T(8,128)(2,1)} %reshape.628), calls=%async_computation.6 | async-start | bytes 2097152 | tf_op jit(solution)/shard_map/all_to_all | solution.py:232
  1177.5 4.9 copy-start.33
  1177.5 76.3 %all-to-all-start.7 = ((bf16[1,8,8,24576]{3,1,0,2:T(8,128)(2,1)}), bf16[1,8,8,24576]{3,1,0,2:T(8,128)(2,1)}, u32[]{:S(2)}, u32[]{:S(2)}) async-start(bf16[1,8,8,24576]{3,1,0,2:T(8,128)(2,1)} %copy.245), calls=%async_computation.7 | async-start | bytes 6291456 | tf_op jit(solution)/shard_map/all_to_all | solution.py:250
  1182.3 364.8 %reduce-scatter.2.cloned.1.call-start = ((), (), s32[]{:S(2)}) async-start(), calls=%async_computation.10 | async-start | bytes 25952256 | tf_op jit(solution)/shard_map/reduce_scatter | solution.py:268
  1184.1 6.6 copy-start.13
  1184.2 6.6 copy-start.86
  1184.2 6.6 copy-start.103
  1184.2 6.6 copy-start.106
  1184.2 6.6 copy-start.113
  1190.8 6.9 copy-start.30
  1214.7 4.8 copy-start.43
  1214.7 4.8 copy-start.55
  1219.6 4.0 copy-start.9
  1219.6 4.0 copy-start.73
  1219.6 4.0 copy-start.93
  1219.6 4.0 copy-start.99
  1219.6 4.0 copy-start.111
  1219.6 4.0 copy-start.125
  1282.8 3.7 copy-start.25
  1286.5 4.0 copy-start.44
  1286.5 4.0 copy-start.66
  1286.5 4.0 copy-start.78
  1286.5 4.0 copy-start.96
  1286.6 4.0 copy-start.109
  1296.7 3.7 copy-start.41
  1302.7 247.3 %copy-start.120 = (s32[96]{0:T(128)S(1)}, s32[96]{0:T(128)}, u32[]{:S(2)}) copy-start(s32[96]{0:T(128)} %copy-done.119) | copy-start | bytes 1156
  1302.7 247.3 %copy-start.121 = (pred[96]{0:T(512)(128)(4,1)S(1)}, pred[96]{0:T(512)(128)(4,1)}, u32[]{:S(2)}) copy-start(pred[96]{0:T(512)(128)(4,1)} %get-tuple-element.756) | copy-start | bytes 292
  1302.8 345.8 %all-gather.5.cloned.1.call-start = ((), (), s32[]{:S(2)}) async-start(), calls=%async_computation.11 | async-start | bytes 12976128 | tf_op jit(solution)/shard_map/all_gather | solution.py:273
  1576.6 47.8 %copy-start.69 = (f32[8,512]{1,0:T(8,128)S(1)}, f32[8,512]{1,0:T(8,128)}, u32[]{:S(2)}) copy-start(f32[8,512]{1,0:T(8,128)} %param.33) | copy-start | bytes 49156
  1576.6 47.8 %copy-start.100 = (f32[8,512]{1,0:T(8,128)S(1)}, f32[8,512]{1,0:T(8,128)}, u32[]{:S(2)}) copy-start(f32[8,512]{1,0:T(8,128)} %param.35) | copy-start | bytes 49156
  1576.6 47.8 %copy-start.101 = (f32[8,512]{1,0:T(8,128)S(1)}, f32[8,512]{1,0:T(8,128)}, u32[]{:S(2)}) copy-start(f32[8,512]{1,0:T(8,128)} %param.34) | copy-start | bytes 49156
  1673.7 9.6 copy-start.26
  1673.7 10.5 copy-start.27
  1683.4 5.6 copy-start.28
  (101 other events, 208.0 us)
Sparse Core Ops, SparseCore 0:
  11.3 153.7 all-gather.2
  1302.9 244.2 reduce-scatter.1
  1551.2 97.3 all-gather.4
where the time goes:
time: 1710 us; the launch traced here: 1700 us
  waiting for transfers between devices  652 us (38%)
  local copies, waits for them, and re-layouts  502 us (29%)
  matrix products  228 us (13%)
  blocking collectives  117 us (7%)
  other arithmetic  104 us (6%)
  loops' own time  47.6 us (3%)
  starting transfers between devices  28.3 us (2%)
  between operations  18 us (1%)
    reduce_scatter x1, waiting for transfers between devices, local(): lax.psum_scatter(dense.reshape(-1, tile_width), ('rows', 'seq'), scatter_...  244 us
    all_gather x1, waiting for transfers between devices, local(): lax.all_gather(master_tiles.astype(jnp.bfloat16), 'seq', axis=0, tiled=True)  148 us
    all_to_all x2, waiting for transfers between devices, local(): lax.all_to_all(outgoing, 'seq', split_axis=0, concat_axis=2, tiled=True)  143 us
    dot_general x104, matrix products, right_product(): lax.dot_general(left, right, (((1,), (1,)), ((), ())), preferred_element_...  98.8 us
    all_to_all x1, blocking collectives, local(): lax.all_to_all(packed_grads.reshape(1, group_rows, seq_devices, positions...  74.5 us
    dot_general x72, matrix products, matmul(): return jnp.dot(left, right, preferred_element_type=jnp.float32)  69.5 us
    dot_general x72, matrix products, left_product(): lax.dot_general(left, right, (((0,), (0,)), ((), ())), preferred_element_...  59.3 us
    unnamed x257, local copies, waits for them, and re-layouts  54.5 us
  transfers between devices with their start and end apart: 10, of which 10 were waited for; matrix products, arithmetic and copies ran while one was open for 7% of the time, Pallas kernels for 0%

commit v1 on v0

--- a/solution.py
+++ b/solution.py
@@ -147,7 +147,17 @@
     matches = (owners[:, None] == seq_index) & (ranks[:, None] == local_slots[None, :])
     chosen = jnp.sum(jnp.where(matches, places[:, None], 0), axis=0)
     present = jnp.any(matches, axis=0)
-    copies = lax.all_gather(master_tiles.astype(jnp.bfloat16), "seq", axis=0, tiled=True)
+    x = master_tiles.astype(jnp.bfloat16)
+    ways = lax.axis_size("seq")
+    up = [(d, (d + 1) % ways) for d in range(ways)]
+    down = [(d, (d - 1) % ways) for d in range(ways)]
+    earlier, later = ([x], [x])
+    for _ in range(ways // 2):
+        earlier.append(lax.ppermute(earlier[-1], "seq", up))
+    for _ in range((ways - 1) // 2):
+        later.append(lax.ppermute(later[-1], "seq", down))
+    line = jnp.concatenate([*earlier[::-1], *later[1:]], axis=0)
+    copies = jnp.roll(line, (lax.axis_index("seq") - ways // 2) * x.shape[0], axis=0)
     weight_tiles = jnp.take(copies, slot_ids, axis=0)
     my_group = seq_index // HEADS
     doc_rows = lax.dynamic_slice_in_dim(segments, my_group * group_rows, group_rows, 0)

time: 1710 us -> 2010 us (1.18)
  matrix products: 228 us -> 403 us
  local copies, waits for them, and re-layouts: 502 us -> 582 us
    ppermute x0 -> x7, waiting for transfers between devices: none -> 160 us  [the longest x4 160 us: local(): earlier.append(lax.ppermute(earlier[-1], 'seq', up))]
    all_gather x1 -> x0, waiting for transfers between devices: 148 us -> none  [local(): lax.all_gather(master_tiles.astype(jnp.bfloat16), 'seq', axis=0, tiled=True)]
    dot_general x72, matrix products: 59.3 us -> 140 us  [left_product(): lax.dot_general(left, right, (((0,), (0,)), ((), ())), preferred_element_...]
    dot_general x104, matrix products: 98.8 us -> 164 us  [right_product(): lax.dot_general(left, right, (((1,), (1,)), ((), ())), preferred_element_...]
    dot_general x72, matrix products: 69.5 us -> 99.7 us  [matmul(): return jnp.dot(left, right, preferred_element_type=jnp.float32)]
    squeeze x16, local copies, waits for them, and re-layouts: 0.42 us -> 26.8 us  [local(): lax.map(backward_item, (arrived, doc_rows, logsums, head_grads))]
    while x80 -> x48, local copies, waits for them, and re-layouts: 24.7 us -> 0.15 us
    dynamic_slice x32, local copies, waits for them, and re-layouts: 0.3 us -> 24.6 us  [local(): attended, logsums = lax.map(forward_item, (arrived, doc_rows))]
  transfers between devices with their start and end apart: 10 -> 16, of which waited for: 10 -> 13; matrix products, arithmetic and copies ran while one was open for 7% -> 6% of each run, Pallas kernels for 0% -> 0%
where the time goes in v1:
time: 2010 us; the launch traced here: 1990 us
  waiting for transfers between devices  665 us (33%)
  local copies, waits for them, and re-layouts  582 us (29%)
  matrix products  403 us (20%)
  other arithmetic  119 us (6%)
  blocking collectives  117 us (6%)
  loops' own time  46.2 us (2%)
  starting transfers between devices  39.4 us (2%)
    reduce_scatter x1, waiting for transfers between devices, local(): lax.psum_scatter(dense.reshape(-1, tile_width), ('rows', 'seq'), scatter_...  244 us
    dot_general x104, matrix products, right_product(): lax.dot_general(left, right, (((1,), (1,)), ((), ())), preferred_element_...  164 us
    ppermute x4, waiting for transfers between devices, local(): earlier.append(lax.ppermute(earlier[-1], 'seq', up))  160 us
    all_to_all x2, waiting for transfers between devices, local(): lax.all_to_all(outgoing, 'seq', split_axis=0, concat_axis=2, tiled=True)  143 us
    dot_general x72, matrix products, left_product(): lax.dot_general(left, right, (((0,), (0,)), ((), ())), preferred_element_...  140 us
    dot_general x72, matrix products, matmul(): return jnp.dot(left, right, preferred_element_type=jnp.float32)  99.7 us
    unnamed x278, local copies, waits for them, and re-layouts  76 us
    all_to_all x1, blocking collectives, local(): lax.all_to_all(packed_grads.reshape(1, group_rows, seq_devices, positions...  74.2 us
  transfers between devices with their start and end apart: 16, of which 13 were waited for; matrix products, arithmetic and copies ran while one was open for 6% of the time, Pallas kernels for 0%

profile of v1, /device:TPU:0, one launch (start us, length us, event | category | flops | bytes accessed | tf_op | source)
XLA Modules:
  0.0 1990.2 jit_solution(779096706371910155)
XLA Ops:
  10.4 27.8 %collective-permute-done = bf16[16,512,128]{2,1,0:T(8,128)(2,1)S(1)} collective-permute-done((bf16[16,512,128]{2,1,0:T(8,128)(2,1)S(1)}, bf16[16,512,128]{2,1,0:T(8,128)(2,1)S(1)}, u32[]{:S(2)}, u32[]{:S(2)}) %collective-permute-start) | collective-permute-done | bytes 2097184 | tf_op jit(solution)/shard_map/ppermute | solution.py:156
  43.0 45.4 %collective-permute-done.1 = bf16[16,512,128]{2,1,0:T(8,128)(2,1)S(1)} collective-permute-done((bf16[16,512,128]{2,1,0:T(8,128)(2,1)S(1)}, bf16[16,512,128]{2,1,0:T(8,128)(2,1)S(1)}, u32[]{:S(2)}, u32[]{:S(2)}) %collective-permute-start.1) | collective-permute-done | bytes 2097184 | tf_op jit(solution)/shard_map/ppermute | solution.py:156
  93.3 46.4 %collective-permute-done.2 = bf16[16,512,128]{2,1,0:T(8,128)(2,1)} collective-permute-done((bf16[16,512,128]{2,1,0:T(8,128)(2,1)S(1)}, bf16[16,512,128]{2,1,0:T(8,128)(2,1)}, u32[]{:S(2)}, u32[]{:S(2)}) %collective-permute-start.2) | collective-permute-done | bytes 2097184 | tf_op jit(solution)/shard_map/ppermute | solution.py:156
  147.3 40.9 %collective-permute-done.3 = bf16[16,512,128]{2,1,0:T(8,128)(2,1)} collective-permute-done((bf16[16,512,128]{2,1,0:T(8,128)(2,1)}, bf16[16,512,128]{2,1,0:T(8,128)(2,1)}, u32[]{:S(2)}, u32[]{:S(2)}) %collective-permute-start.3) | collective-permute-done | bytes 2097184 | tf_op jit(solution)/shard_map/ppermute | solution.py:156
  213.2 6.8 constant_dynamic-slice_fusion.6
  220.0 12.7 gather_fusion
  232.7 6.5 broadcast_select_fusion
  257.6 10.0 copy.210
  267.5 10.4 reshape.599
  281.9 71.4 %all-to-all-done = bf16[8,8,24576]{2,1,0:T(8,128)(2,1)S(1)} async-done(((bf16[8,8,24576]{2,1,0:T(8,128)(2,1)}), bf16[8,8,24576]{2,1,0:T(8,128)(2,1)S(1)}, u32[]{:S(2)}, u32[]{:S(2)}) %all-to-all-start) | async-done | bytes 3145760 | tf_op jit(solution)/shard_map/all_to_all | solution.py:176
  356.8 10.5 reshape.600
  367.3 7.7 copy.212
  375.8 78.8 %while.99 = (s32[]{:T(128)}, bf16[8,1024,64]{2,1,0:T(8,128)(2,1)S(1)}, f32[8,1024]{1,0:T(8,128)}, bf16[8,1024,3,64]{3,1,2,0:T(8,128)(2,1)}, s32[8,1024]{1,0:T(8,...) while((s32[]{:T(128)}, ...), condition=%wide.region_8.9_spmd, body=%wide.region_3.8_spmd.sunk | while | flops 139492864 | bytes 9431484 | solution.py:185
  519.2 10.0 copy.220
  529.2 10.4 reshape.610
  544.3 71.5 %all-to-all-done.2 = bf16[8,8,24576]{2,1,0:T(8,128)(2,1)} async-done(((bf16[8,8,24576]{2,1,0:T(8,128)(2,1)}), bf16[8,8,24576]{2,1,0:T(8,128)(2,1)}, u32[]{:S(2)}, u32[]{:S(2)}) %all-to-all-start.2) | async-done | bytes 3145760 | tf_op jit(solution)/shard_map/all_to_all | solution.py:176
  621.1 10.5 reshape.611
  631.6 7.7 copy.222
  640.9 74.6 %while.101 = (s32[]{:T(128)}, bf16[8,1024,64]{2,1,0:T(8,128)(2,1)}, f32[8,1024]{1,0:T(8,128)S(1)}, bf16[8,1024,3,64]{3,1,2,0:T(8,128)(2,1)}, s32[8,1024]{1,0:T(8...) while((s32[]{:T(128)}, bf16[8,1024,64]{2,1,0:T(8,128)(2,1)}, ...), condition=%wide.region_18.19_spmd, body=%wide.region_13.18_spmd.sunk | while | flops 139492864 | bytes 9300412 | solution.py:185
  670.9 6.3 while.107
  740.5 10.4 all-to-all-done.3
  760.7 6.5 fusion.71
  767.2 7.8 fusion.63
  790.7 26.5 %all-to-all-done.4 = bf16[8,8,8192]{2,1,0:T(8,128)(2,1)S(1)} async-done(((bf16[8,8,8192]{2,1,0:T(8,128)(2,1)}), bf16[8,8,8192]{2,1,0:T(8,128)(2,1)S(1)}, u32[]{:S(2)}, u32[]{:S(2)}) %all-to-all-start.4) | async-done | bytes 1048608 | tf_op jit(solution)/shard_map/all_to_all | solution.py:242
  823.1 210.7 %while.103 = (s32[]{:T(128)}, bf16[8,1024,3,64]{1,3,2,0:T(8,128)(2,1)}, bf16[8,1024,3,64]{3,1,2,0:T(8,128)(2,1)}, s32[8,1024]{1,0:T(8,128)}, f32[8,1024]{1,0:T(8...) while((s32[]{:T(128)}, ...), condition=%wide.region_27.28_spmd, body=%wide.region_23.27_spmd.sunk | while | flops 342982144 | bytes 22319684 | solution.py:259
  827.7 19.7 while.108
  854.1 19.7 while.108
  880.4 19.7 while.108
  906.7 19.7 while.108
  933.1 19.7 while.108
  959.4 19.7 while.108
  985.7 19.7 while.108
  1012.1 19.7 while.108
  1033.8 12.6 copy.235
  1046.4 9.2 reshape.624
  1057.3 74.2 %all_to_all.120 = bf16[1,8,8,24576]{3,1,0,2:T(8,128)(2,1)S(1)} all-to-all(bf16[1,8,8,24576]{3,1,0,2:T(8,128)(2,1)S(1)} %copy.236), channel_id=1, replica_groups=mesh['rows'=4,'seq'=8] {'seq'}, dimensions={2} | all-to-all | bytes 6291456 | tf_op jit(solution)/shard_map/all_to_all | solution.py:260
  1131.6 8.7 reshape.625
  1140.3 8.0 copy.237
  1164.3 10.4 fusion.56
  1197.4 26.5 %all-to-all-done.6 = bf16[8,8,8192]{2,1,0:T(8,128)(2,1)S(1)} async-done(((bf16[8,8,8192]{2,1,0:T(8,128)(2,1)}), bf16[8,8,8192]{2,1,0:T(8,128)(2,1)S(1)}, u32[]{:S(2)}, u32[]{:S(2)}) %all-to-all-start.6) | async-done | bytes 1048608 | tf_op jit(solution)/shard_map/all_to_all | solution.py:242
  1229.8 215.8 %while.105 = (s32[]{:T(128)}, bf16[8,1024,3,64]{1,3,2,0:T(8,128)(2,1)}, bf16[8,1024,3,64]{3,1,2,0:T(8,128)(2,1)}, s32[8,1024]{1,0:T(8,128)}, f32[8,1024]{1,0:T(8...) while((s32[]{:T(128)}, ...), condition=%wide.region_36.37_spmd, body=%wide.region_32.36_spmd.sunk | while | flops 342982144 | bytes 22057484 | solution.py:259
  1235.1 19.7 while.109
  1262.1 19.6 while.109
  1289.1 19.7 while.109
  1316.0 19.6 while.109
  1343.0 19.7 while.109
  1370.0 19.6 while.109
  1397.0 19.7 while.109
  1424.0 19.6 while.109
  1445.6 12.6 copy.244
  1458.2 9.2 reshape.630
  1477.4 6.5 copy.267
  1484.0 6.9 convolution_bitcast_fusion
  1493.5 9.2 fusion.106
  1521.3 25.6 %all-to-all-done.7 = bf16[1,8,8,24576]{3,1,0,2:T(8,128)(2,1)} async-done(((bf16[1,8,8,24576]{3,1,0,2:T(8,128)(2,1)}), bf16[1,8,8,24576]{3,1,0,2:T(8,128)(2,1)}, u32[]{:S(2)}, u32[]{:S(2)}) %all-to-all-start.7) | async-done | bytes 3145760 | tf_op jit(solution)/shard_map/all_to_all | solution.py:260
  1546.9 10.6 reshape.631
  1557.5 9.3 copy.246
  1595.7 244.2 %reduce-scatter.2.cloned.1.call-done = f32[1536,128]{1,0:T(8,128)} async-done(((f32[49152,128]{1,0:T(8,128)}), f32[1536,128]{1,0:T(8,128)}) %reduce-scatter.2.cloned.1.call-update) | async-done | bytes 786448 | tf_op jit(solution)/shard_map/reduce_scatter | solution.py:278
  1843.1 8.7 fusion.91
  1872.6 42.6 %all-reduce = (f32[]{:T(128)}, f32[8,512]{1,0:T(8,128)S(1)}) all-reduce(f32[]{:T(128)} %get-tuple-element.743, f32[8,512]{1,0:T(8,128)S(1)} %concatenate.30), channel_id=1, replica_groups=mesh['rows'=4,'seq'=8] {'rows','seq'}, use_global_device_ids=true, to_apply=%region_43.44 | all-reduce | flops 4097 | bytes 32776 | tf_op jit(solution)/shard_map/psum | solution.py:281
  1917.9 23.5 %all-gather.2.cloned.1.call-done = bf16[49152,128]{1,0:T(8,128)(2,1)} async-done(((bf16[1536,128]{1,0:T(8,128)(2,1)}), bf16[49152,128]{1,0:T(8,128)(2,1)}) %all-gather.2.cloned.1.call-update) | async-done | bytes 12582928 | tf_op jit(solution)/shard_map/all_gather | solution.py:283
  1941.3 14.2 convert.25
  1955.5 11.0 gather_fusion.1
  1966.6 9.6 fusion.133
  (1348 shorter events, 967.6 us)
Async XLA Ops:
  7.2 132.5 %copy-start.7 = (f32[8,128,512]{2,1,0:T(8,128)S(1)}, f32[8,128,512]{2,1,0:T(8,128)}, u32[]{:S(2)}) copy-start(f32[8,128,512]{2,1,0:T(8,128)} %param.26) | copy-start | bytes 6291460
  9.9 130.0 %copy-start.120 = (s32[96]{0:T(128)S(1)}, s32[96]{0:T(128)}, u32[]{:S(2)}) copy-start(s32[96]{0:T(128)} %param.29) | copy-start | bytes 1156
  9.9 28.3 %collective-permute-start = (bf16[16,512,128]{2,1,0:T(8,128)(2,1)S(1)}, bf16[16,512,128]{2,1,0:T(8,128)(2,1)S(1)}, u32[]{:S(2)}, u32[]{:S(2)}) collective-permute-start(bf16[16,512,128]{2,1,0:T(8,128)(2,1)S(1)} %convert_element_type.116), channel_id=1, source_target_pairs={{0,1},{1,2},{2,3},{3,4},{4,5},{5,6},{6,7},{7,0},{8,9},{9,10},{10,1... | collective-permute-start | bytes 6291464 | tf_op jit(solution)/shard_map/ppermute | solution.py:156
  39.5 49.0 %collective-permute-start.1 = (bf16[16,512,128]{2,1,0:T(8,128)(2,1)S(1)}, bf16[16,512,128]{2,1,0:T(8,128)(2,1)S(1)}, u32[]{:S(2)}, u32[]{:S(2)}) collective-permute-start(bf16[16,512,128]{2,1,0:T(8,128)(2,1)S(1)} %collective-permute-done), channel_id=1, source_target_pairs={{0,1},{1,2},{2,3},{3,4},{4,5},{5,6},{6,7},{7,0},{8,9},{9,10},{10,1... | collective-permute-start | bytes 6291464 | tf_op jit(solution)/shard_map/ppermute | solution.py:156
  39.5 50.3 %collective-permute-start.4 = (bf16[16,512,128]{2,1,0:T(8,128)(2,1)S(1)}, bf16[16,512,128]{2,1,0:T(8,128)(2,1)}, u32[]{:S(2)}, u32[]{:S(2)}) collective-permute-start(bf16[16,512,128]{2,1,0:T(8,128)(2,1)S(1)} %convert_element_type.116), channel_id=1, source_target_pairs={{0,7},{1,0},{2,1},{3,2},{4,3},{5,4},{6,5},{7,6},{8,15},{9,8},{10,9... | collective-permute-start | bytes 6291464 | tf_op jit(solution)/shard_map/ppermute | solution.py:158
  89.8 49.9 %collective-permute-start.2 = (bf16[16,512,128]{2,1,0:T(8,128)(2,1)S(1)}, bf16[16,512,128]{2,1,0:T(8,128)(2,1)}, u32[]{:S(2)}, u32[]{:S(2)}) collective-permute-start(bf16[16,512,128]{2,1,0:T(8,128)(2,1)S(1)} %collective-permute-done.1), channel_id=1, source_target_pairs={{0,1},{1,2},{2,3},{3,4},{4,5},{5,6},{6,7},{7,0},{8,9},{9,10},{10,1... | collective-permute-start | bytes 6291464 | tf_op jit(solution)/shard_map/ppermute | solution.py:156
  89.8 51.9 %collective-permute-start.5 = (bf16[16,512,128]{2,1,0:T(8,128)(2,1)}, bf16[16,512,128]{2,1,0:T(8,128)(2,1)}, u32[]{:S(2)}, u32[]{:S(2)}) collective-permute-start(bf16[16,512,128]{2,1,0:T(8,128)(2,1)} %collective-permute-done.4), channel_id=1, source_target_pairs={{0,7},{1,0},{2,1},{3,2},{4,3},{5,4},{6,5},{7,6},{8,15},{9,8},{10,9... | collective-permute-start | bytes 6291464 | tf_op jit(solution)/shard_map/ppermute | solution.py:158
  139.7 48.4 %collective-permute-start.3 = (bf16[16,512,128]{2,1,0:T(8,128)(2,1)}, bf16[16,512,128]{2,1,0:T(8,128)(2,1)}, u32[]{:S(2)}, u32[]{:S(2)}) collective-permute-start(bf16[16,512,128]{2,1,0:T(8,128)(2,1)} %collective-permute-done.2), channel_id=1, source_target_pairs={{0,1},{1,2},{2,3},{3,4},{4,5},{5,6},{6,7},{7,0},{8,9},{9,10},{10,1... | collective-permute-start | bytes 6291464 | tf_op jit(solution)/shard_map/ppermute | solution.py:156
  139.7 5.6 copy-start.70
  140.1 7.1 copy-start.121
  141.7 58.6 %collective-permute-start.6 = (bf16[16,512,128]{2,1,0:T(8,128)(2,1)}, bf16[16,512,128]{2,1,0:T(8,128)(2,1)}, u32[]{:S(2)}, u32[]{:S(2)}) collective-permute-start(bf16[16,512,128]{2,1,0:T(8,128)(2,1)} %collective-permute-done.5), channel_id=1, source_target_pairs={{0,7},{1,0},{2,1},{3,2},{4,3},{5,4},{6,5},{7,6},{8,15},{9,8},{10,9... | collective-permute-start | bytes 6291464 | tf_op jit(solution)/shard_map/ppermute | solution.py:158
  145.9 350.1 %copy-start.99 = (f32[1,512]{1,0:T(1,128)}, f32[1,512]{1,0:T(1,128)S(1)}, u32[]{:S(2)}) copy-start(f32[1,512]{1,0:T(1,128)S(1)} %get-tuple-element.748) | copy-start | bytes 6148
  145.9 350.1 %copy-start.112 = (f32[1,512]{1,0:T(1,128)}, f32[1,512]{1,0:T(1,128)S(1)}, u32[]{:S(2)}) copy-start(f32[1,512]{1,0:T(1,128)S(1)} %get-tuple-element.747) | copy-start | bytes 6148
  239.3 4.6 copy-start.6
  277.9 75.4 %all-to-all-start = ((bf16[8,8,24576]{2,1,0:T(8,128)(2,1)}), bf16[8,8,24576]{2,1,0:T(8,128)(2,1)S(1)}, u32[]{:S(2)}, u32[]{:S(2)}) async-start(bf16[8,8,24576]{2,1,0:T(8,128)(2,1)} %reshape.599), calls=%async_computation | async-start | bytes 6291456 | tf_op jit(solution)/shard_map/all_to_all | solution.py:176
  457.9 30.1 %all-to-all-start.1 = ((bf16[1,8,8,8192]{3,1,0,2:T(8,128)(2,1)}), bf16[1,8,8,8192]{3,1,0,2:T(8,128)(2,1)S(1)}, u32[]{:S(2)}, u32[]{:S(2)}) async-start(bf16[1,8,8,8192]{3,1,0,2:T(8,128)(2,1)} %copy.213), calls=%async_computation.1 | async-start | bytes 2097152 | tf_op jit(solution)/shard_map/all_to_all | solution.py:187
  463.4 30.0 %copy-start.1 = (f32[1024,512]{0,1:T(8,128)}, f32[1024,512]{0,1:T(8,128)S(1)}, u32[]{:S(2)}) copy-start(f32[1024,512]{0,1:T(8,128)S(1)} %copy.262) | copy-start | bytes 6291460
  495.6 5.1 copy-start.8
  495.6 5.0 copy-start.73
  495.9 4.7 copy-start.81
  495.9 4.7 copy-start.93
  504.3 251.9 %copy-start.3 = (f32[1024,512]{0,1:T(8,128)}, f32[1024,512]{0,1:T(8,128)S(1)}, u32[]{:S(2)}) copy-start(f32[1024,512]{0,1:T(8,128)S(1)} %get-tuple-element.760) | copy-start | bytes 6291460
  539.6 76.2 %all-to-all-start.2 = ((bf16[8,8,24576]{2,1,0:T(8,128)(2,1)}), bf16[8,8,24576]{2,1,0:T(8,128)(2,1)}, u32[]{:S(2)}, u32[]{:S(2)}) async-start(bf16[8,8,24576]{2,1,0:T(8,128)(2,1)} %reshape.610), calls=%async_computation.2 | async-start | bytes 6291456 | tf_op jit(solution)/shard_map/all_to_all | solution.py:176
  720.4 30.5 %all-to-all-start.3 = ((bf16[1,8,8,8192]{3,1,0,2:T(8,128)(2,1)}), bf16[1,8,8,8192]{3,1,0,2:T(8,128)(2,1)S(1)}, u32[]{:S(2)}, u32[]{:S(2)}) async-start(bf16[1,8,8,8192]{3,1,0,2:T(8,128)(2,1)} %copy.223), calls=%async_computation.3 | async-start | bytes 2097152 | tf_op jit(solution)/shard_map/all_to_all | solution.py:187
  758.3 20.3 %copy-start.13 = (f32[1024,512]{0,1:T(8,128)}, f32[1024,512]{0,1:T(8,128)S(1)}, u32[]{:S(2)}) copy-start(f32[1024,512]{0,1:T(8,128)S(1)} %get-tuple-element.762) | copy-start | bytes 6291460
  758.4 20.2 %copy-start.87 = (f32[1024]{0:T(1024)}, f32[1024]{0:T(1024)S(1)}, u32[]{:S(2)}) copy-start(f32[1024]{0:T(1024)S(1)} %broadcast_multiply_fusion.1) | copy-start | bytes 12292
  758.7 19.9 %copy-start.104 = (f32[1024]{0:T(1024)}, f32[1024]{0:T(1024)S(1)}, u32[]{:S(2)}) copy-start(f32[1024]{0:T(1024)S(1)} %fusion.118) | copy-start | bytes 12292
  760.7 6.5 copy-start.49
  760.7 6.5 copy-start.58
  767.2 7.9 copy-start.128
  787.0 30.3 %all-to-all-start.4 = ((bf16[8,8,8192]{2,1,0:T(8,128)(2,1)}), bf16[8,8,8192]{2,1,0:T(8,128)(2,1)S(1)}, u32[]{:S(2)}, u32[]{:S(2)}) async-start(bf16[8,8,8192]{2,1,0:T(8,128)(2,1)} %reshape.622), calls=%async_computation.4 | async-start | bytes 2097152 | tf_op jit(solution)/shard_map/all_to_all | solution.py:242
  823.1 4.6 copy-start.68
  849.5 4.6 copy-start.68
  875.8 4.6 copy-start.68
  902.1 4.6 copy-start.68
  928.5 4.6 copy-start.68
  954.8 4.6 copy-start.68
  981.1 4.6 copy-start.68
  1007.5 4.6 copy-start.68
  1148.3 6.3 copy-start.30
  1164.3 10.4 copy-start.22
  1164.3 10.4 copy-start.51
  1174.6 4.2 copy-start.126
  1193.8 30.1 %all-to-all-start.6 = ((bf16[8,8,8192]{2,1,0:T(8,128)(2,1)}), bf16[8,8,8192]{2,1,0:T(8,128)(2,1)S(1)}, u32[]{:S(2)}, u32[]{:S(2)}) async-start(bf16[8,8,8192]{2,1,0:T(8,128)(2,1)} %reshape.628), calls=%async_computation.6 | async-start | bytes 2097152 | tf_op jit(solution)/shard_map/all_to_all | solution.py:242
  1470.8 4.7 copy-start.34
  1470.8 76.1 %all-to-all-start.7 = ((bf16[1,8,8,24576]{3,1,0,2:T(8,128)(2,1)}), bf16[1,8,8,24576]{3,1,0,2:T(8,128)(2,1)}, u32[]{:S(2)}, u32[]{:S(2)}) async-start(bf16[1,8,8,24576]{3,1,0,2:T(8,128)(2,1)} %copy.245), calls=%async_computation.7 | async-start | bytes 6291456 | tf_op jit(solution)/shard_map/all_to_all | solution.py:260
  1475.4 364.6 %reduce-scatter.2.cloned.1.call-start = ((), (), s32[]{:S(2)}) async-start(), calls=%async_computation.9 | async-start | bytes 25952256 | tf_op jit(solution)/shard_map/reduce_scatter | solution.py:278
  1477.4 6.6 copy-start.14
  1477.4 6.6 copy-start.88
  1477.4 6.6 copy-start.105
  1477.4 6.6 copy-start.108
  1477.4 6.6 copy-start.115
  1484.0 6.9 copy-start.31
  1507.9 4.8 copy-start.45
  1507.9 4.8 copy-start.57
  1595.6 247.3 %copy-start.122 = (s32[96]{0:T(128)S(1)}, s32[96]{0:T(128)}, u32[]{:S(2)}) copy-start(s32[96]{0:T(128)} %copy-done.121) | copy-start | bytes 1156
  1595.6 247.3 %copy-start.123 = (pred[96]{0:T(512)(128)(4,1)S(1)}, pred[96]{0:T(512)(128)(4,1)}, u32[]{:S(2)}) copy-start(pred[96]{0:T(512)(128)(4,1)} %get-tuple-element.756) | copy-start | bytes 292
  1595.6 345.7 %all-gather.2.cloned.1.call-start = ((), (), s32[]{:S(2)}) async-start(), calls=%async_computation.10 | async-start | bytes 12976128 | tf_op jit(solution)/shard_map/all_gather | solution.py:283
  1869.6 47.6 %copy-start.71 = (f32[8,512]{1,0:T(8,128)S(1)}, f32[8,512]{1,0:T(8,128)}, u32[]{:S(2)}) copy-start(f32[8,512]{1,0:T(8,128)} %param.33) | copy-start | bytes 49156
  1869.6 47.6 %copy-start.102 = (f32[8,512]{1,0:T(8,128)S(1)}, f32[8,512]{1,0:T(8,128)}, u32[]{:S(2)}) copy-start(f32[8,512]{1,0:T(8,128)} %param.35) | copy-start | bytes 49156
  1869.6 47.6 %copy-start.103 = (f32[8,512]{1,0:T(8,128)S(1)}, f32[8,512]{1,0:T(8,128)}, u32[]{:S(2)}) copy-start(f32[8,512]{1,0:T(8,128)} %param.34) | copy-start | bytes 49156
  1966.6 9.6 copy-start.27
  1966.6 10.5 copy-start.28
  1976.2 5.6 copy-start.29
  (95 other events, 242.1 us)
Sparse Core Ops, SparseCore 0:
  1595.8 244.1 reduce-scatter.1
  1843.9 97.3 all-gather.1
